TPU v7x, 1024 devices: a whole 8x8x8 slice. The times are simulated.
1024 devices in a mesh: space: 64 (over y, x), lane: 16 (over z, core).
Axes of the slice: x: 8, y: 8, z: 8, core: 2. Of those that a mesh axis runs over, the one named last changes fastest.
Arguments:
- positions: float32 [2048, 3, 544], P('space'), may hold values from -6 to 6
- bend_op: float32 [544, 544], replicated, may hold values from -0.25 to 0.25
- send_list: int32 [64, 64], P('space'), may hold values from 0 to 31
- task_target: int32 [1024, 12], P(('space', 'lane')), may hold values from 0 to 31, as said below
- task_source: int32 [1024, 12], P(('space', 'lane')), may hold values from 0 to 95, as said below
- task_count: int32 [1024], P(('space', 'lane')), may hold values from 4 to 12, as said below
Outputs:
- moved_positions: float32 [2048, 3, 544], P(('space', 'lane'))
- velocity: float32 [2048, 3, 544], P(('space', 'lane'))
Inputs may be any that keep to these rules, and one draw needn't show every extreme that they name: `task_target`: slots at or beyond the list's task_count hold 0. `task_source`: slots at or beyond the list's task_count hold 0. Every received cell of an owner is the source of at least one live slot of that owner. `task_count`: in each owner exactly one lane has 12 live slots; every other lane has at most 7.
All inputs are finite; a program needn't handle non-finite values.
Results may differ from a plain program's by a relative error of at most 0.00015.
Values sent between devices are 32-bit elements; how exact they have to be, the bound alone decides.
A program may use at most 32 MiB of HBM per device.

v0:
```python
import math

import jax
import jax.numpy as jnp
from jax import lax
from jax.sharding import PartitionSpec as P

G = 1
TASK_CAP = 12
ITERS = 2


REGULARIZE = 0.25
TIME_STEP = 0.5


def sent_together(arrays, axis, dim, along):
    widths = [math.prod(a.shape[along:]) for a in arrays]
    both = jnp.concatenate(
        [a.reshape(*a.shape[:along], w) for a, w in zip(arrays, widths)], axis=along
    )
    out = lax.all_gather(both, axis, axis=dim, tiled=True)
    blocks = jnp.split(out, [sum(widths[:k]) for k in range(1, len(widths))], axis=along)
    return tuple((b.reshape(*out.shape[:along], *a.shape[along:]) for a, b in zip(arrays, blocks)))


def in_blocks(value, dim, peers):
    before, after = (value.shape[:dim], value.shape[dim + 1 :])
    return jnp.moveaxis(value.reshape(*before, peers, -1, *after), dim, 0)


def sum_at_owner(value, axis, dim):
    blocks = in_blocks(value, dim, lax.axis_size(axis))
    arrived = lax.all_to_all(blocks, axis, split_axis=0, concat_axis=0, tiled=True)
    return arrived.sum(axis=0)


def laid_out(blocks, dim):
    blocks = jnp.moveaxis(blocks, 0, dim)
    dims = blocks.shape
    return blocks.reshape(*dims[:dim], dims[dim] * dims[dim + 1], *dims[dim + 2 :])


def copy_for_each(value, axis):
    peers = lax.axis_size(axis)
    return lax.all_to_all(
        jnp.broadcast_to(value[None], (peers, *value.shape)), axis, 0, 0, tiled=True
    )


def collect(value, axis, dim):
    return laid_out(copy_for_each(value, axis), dim)


def stokes_tile(target_pos, source_pos, source_force):
    off_x = target_pos[0][:, None] - source_pos[0][None, :]
    off_y = target_pos[1][:, None] - source_pos[1][None, :]
    off_z = target_pos[2][:, None] - source_pos[2][None, :]
    distance_sq = off_x * off_x + off_y * off_y + off_z * off_z
    inverse = lax.rsqrt(distance_sq + REGULARIZE)
    inverse_cube = inverse * inverse * inverse
    projected = (
        off_x * source_force[0][None, :]
        + off_y * source_force[1][None, :]
        + off_z * source_force[2][None, :]
    )
    weight_direct = (distance_sq + 2.0 * REGULARIZE) * inverse_cube
    weight_tensor = projected * inverse_cube
    comp_x = jnp.sum(weight_direct * source_force[0][None, :] + weight_tensor * off_x, axis=1)
    comp_y = jnp.sum(weight_direct * source_force[1][None, :] + weight_tensor * off_y, axis=1)
    comp_z = jnp.sum(weight_direct * source_force[2][None, :] + weight_tensor * off_z, axis=1)
    return jnp.stack([comp_x, comp_y, comp_z], axis=0) / source_pos.shape[1]


def bending(current, bend_op):
    flattened = current.reshape(-1, current.shape[-1])
    return jnp.dot(
        flattened, bend_op, precision=lax.Precision.HIGHEST, preferred_element_type=jnp.float32
    ).reshape(current.shape)


def tile_batch(pool_pos, pool_frc, slot_targets, slot_sources, live_mask):
    target_rows = pool_pos[slot_targets]
    source_rows = pool_pos[slot_sources]
    force_rows = pool_frc[slot_sources]

    def single(bundle):
        return stokes_tile(bundle[0], bundle[1], bundle[2])

    tiles = lax.map(single, (target_rows, source_rows, force_rows))
    return tiles * live_mask.astype(jnp.float32)[:, None, None]


def shards(positions, bend_op, send_list, task_target, task_source, task_count):
    owners = lax.axis_size("space")
    lane_count = lax.axis_size("lane")
    lane_index = lax.axis_index("lane")
    cells_owner = positions.shape[0]
    points = positions.shape[2]
    share_rows = cells_owner // lane_count
    every_target, every_source, every_count = sent_together(
        (task_target, task_source, task_count), "lane", 0, 1
    )
    live_slots = (jnp.arange(TASK_CAP)[None, :] < every_count[:, None]).reshape(-1)
    live_order = jnp.argsort(jnp.where(live_slots, 0, 1), stable=True)
    flat_targets = every_target.reshape(-1)[live_order]
    flat_sources = every_source.reshape(-1)[live_order]
    task_total = jnp.sum(every_count)
    my_tasks = (task_total - lane_index + lane_count - 1) // lane_count
    slot_cap = (TASK_CAP + 7 * (lane_count - 1) + lane_count - 1) // lane_count
    slot_range = jnp.arange(slot_cap, dtype=jnp.int32)
    picks = jnp.minimum(lane_index + lane_count * slot_range, flat_targets.shape[0] - 1)
    slot_targets = flat_targets[picks]
    slot_sources = flat_sources[picks]
    live_mask = slot_range < my_tasks
    slot_targets = jnp.where(live_mask, slot_targets, 0)
    slot_sources = jnp.where(live_mask, slot_sources, 0)
    cell_ids = jnp.arange(cells_owner, dtype=jnp.int32)
    matching = ((cell_ids[:, None] == slot_targets[None, :]) & live_mask[None, :]).astype(
        jnp.float32
    )
    current = positions
    moved = positions[:share_rows]
    velocity = jnp.zeros_like(moved)
    for iteration in range(ITERS):
        forces = bending(current, bend_op)
        packed = jnp.concatenate([current, forces], axis=1).reshape(cells_owner, 6 * points)
        outgoing = packed[send_list[0]].reshape(owners, G, 6 * points)
        incoming = lax.all_to_all(outgoing, "space", split_axis=0, concat_axis=0, tiled=True)
        pool_rows = jnp.concatenate([packed, incoming.reshape(-1, 6 * points)], axis=0).reshape(
            -1, 2, 3, points
        )
        pool_pos = pool_rows[:, 0]
        pool_frc = pool_rows[:, 1]
        tiles = tile_batch(pool_pos, pool_frc, slot_targets, slot_sources, live_mask)
        partial_value = jnp.dot(
            matching,
            tiles.reshape(-1, 3 * points),
            precision=lax.Precision.HIGHEST,
            preferred_element_type=jnp.float32,
        ).reshape(cells_owner, 3, points)
        velocity = sum_at_owner(partial_value, "lane", 0)
        moved = (
            lax.dynamic_slice_in_dim(current, lane_index * share_rows, share_rows, 0)
            + TIME_STEP * velocity
        )
        if iteration + 1 < ITERS:
            current = collect(moved, "lane", 0)
    return (moved, velocity)


def solution(mesh):
    in_specs = (
        P("space", None, None),
        P(),
        P("space", None),
        P(("space", "lane"), None),
        P(("space", "lane"), None),
        P(("space", "lane")),
    )
    out_specs = (P(("space", "lane"), None, None), P(("space", "lane"), None, None))
    return jax.shard_map(shards, mesh=mesh, in_specs=in_specs, out_specs=out_specs, check_vma=False)
```

profile of v0, /device:TPU:1, one launch (start us, length us, event | category | flops | bytes accessed | tf_op | source)
XLA Modules:
  0.0 212.8 jit_solution(3644636599831770964)
XLA Ops:
  7.4 14.0 %all-to-all-start = ((f32[64,1,3264]{2,1,0:T(1,128)}), f32[64,1,3264]{2,1,0:T(1,128)S(1)}, u32[]{:S(2)}, u32[]{:S(2)}) async-start(f32[64,1,3264]{2,1,0:T(1,128)} %copy.49), calls=%async_computation | async-start | bytes 1703936 | tf_op jit(solution)/shard_map/all_to_all | solution.py:129
  22.2 30.5 %all-gather = s32[16,1,25]{2,1,0:T(1,128)S(1)} all-gather(s32[1,1,25]{2,1,0:T(1,128)S(1)} %add_bitcast_fusion), channel_id=1, replica_groups=mesh['space'=64,'lane'=16] {'lane'}, dimensions={0}, use_global_device_ids=true | all-gather | bytes 1700 | tf_op jit(solution)/shard_map/all_gather | solution.py:22
  54.5 3.2 %sort.17 = (s32[192]{0:T(256)}, s32[192]{0:T(256)S(1)}) sort(s32[192]{0:T(256)S(1)} %select_n.96, s32[192]{0:T(256)S(1)} %iota.40), dimensions={0}, to_apply=%region_1.2 | sort | flops 1536 | bytes 3072 | tf_op jit(solution)/shard_map/jit(argsort)/sort | solution.py:105
  63.5 3.1 %reduce.20 = f32[64,3264]{1,0:T(8,128)} reduce(f32[64,1,3264]{2,1,0:T(1,128)S(1)} %all-to-all-done, f32[]{:T(128)} %constant.110), dimensions={1}, to_apply=%all_to_all.15.reduce_sub_computation | reduce | bytes 1671172 | tf_op jit(solution)/shard_map/all_to_all | solution.py:129
  73.5 18.5 %while.20 = (s32[]{:T(128)}, f32[8,3,544]{2,1,0:T(4,128)S(1)}, f32[8,3,544]{2,1,0:T(4,128)S(1)}, f32[8,3,544]{2,1,0:T(4,128)S(1)}, f32[8,3,544]{2,1,0:T(4,128)S(1)}, /*index=5*/s32[]{:T(128)}, s32[]{:T(128)}, s32[]{}, s32[]{}) while((s32[]{:T(128)}, f32[8,3,544]{2,1,0:T(4,128)S(1)}, f32[8,3,544]{2,1,0:T(4,128)S(1)}, ...), condition=%wide.region_6.7_spmd, body=%wide.region_2.6_spmd.sunk | while | flops 9177284 | bytes 96401 | solution.py:90
  80.6 2.1 %fusion.63 = (f32[544]{0:T(1024)S(1)}, f32[544]{0:T(1024)S(1)}, f32[544]{0:T(1024)S(1)}) fusion(f32[544]{0:T(1024)S(1)} %get-tuple-element.209, f32[544]{0:T(1024)S(1)} %get-tuple-element.210, f32[544]{0:T(1024)S(1)} %get-tuple-element.211, f32[544]{0:T(1024)S(1)} %get-tuple-element.212, f32[544]{0:T(1024)S(1)} %get-tuple-element.213, ...), kind=kLoop, calls=%fused_computation.28.clone.1 | loop fusion | flops 9172384 | bytes 26112 | tf_op jit(solution)/shard_map/while/body/eval_jaxpr/reduce_sum | solution.py:69
  82.9 2.1 %fusion.63 = (f32[544]{0:T(1024)S(1)}, f32[544]{0:T(1024)S(1)}, f32[544]{0:T(1024)S(1)}) fusion(f32[544]{0:T(1024)S(1)} %get-tuple-element.209, f32[544]{0:T(1024)S(1)} %get-tuple-element.210, f32[544]{0:T(1024)S(1)} %get-tuple-element.211, f32[544]{0:T(1024)S(1)} %get-tuple-element.212, f32[544]{0:T(1024)S(1)} %get-tuple-element.213, ...), kind=kLoop, calls=%fused_computation.28.clone.1 | loop fusion | flops 9172384 | bytes 26112 | tf_op jit(solution)/shard_map/while/body/eval_jaxpr/reduce_sum | solution.py:69
  85.2 2.1 %fusion.63 = (f32[544]{0:T(1024)S(1)}, f32[544]{0:T(1024)S(1)}, f32[544]{0:T(1024)S(1)}) fusion(f32[544]{0:T(1024)S(1)} %get-tuple-element.209, f32[544]{0:T(1024)S(1)} %get-tuple-element.210, f32[544]{0:T(1024)S(1)} %get-tuple-element.211, f32[544]{0:T(1024)S(1)} %get-tuple-element.212, f32[544]{0:T(1024)S(1)} %get-tuple-element.213, ...), kind=kLoop, calls=%fused_computation.28.clone.1 | loop fusion | flops 9172384 | bytes 26112 | tf_op jit(solution)/shard_map/while/body/eval_jaxpr/reduce_sum | solution.py:69
  87.6 2.1 %fusion.63 = (f32[544]{0:T(1024)S(1)}, f32[544]{0:T(1024)S(1)}, f32[544]{0:T(1024)S(1)}) fusion(f32[544]{0:T(1024)S(1)} %get-tuple-element.209, f32[544]{0:T(1024)S(1)} %get-tuple-element.210, f32[544]{0:T(1024)S(1)} %get-tuple-element.211, f32[544]{0:T(1024)S(1)} %get-tuple-element.212, f32[544]{0:T(1024)S(1)} %get-tuple-element.213, ...), kind=kLoop, calls=%fused_computation.28.clone.1 | loop fusion | flops 9172384 | bytes 26112 | tf_op jit(solution)/shard_map/while/body/eval_jaxpr/reduce_sum | solution.py:69
  89.9 2.1 %fusion.63 = (f32[544]{0:T(1024)S(1)}, f32[544]{0:T(1024)S(1)}, f32[544]{0:T(1024)S(1)}) fusion(f32[544]{0:T(1024)S(1)} %get-tuple-element.209, f32[544]{0:T(1024)S(1)} %get-tuple-element.210, f32[544]{0:T(1024)S(1)} %get-tuple-element.211, f32[544]{0:T(1024)S(1)} %get-tuple-element.212, f32[544]{0:T(1024)S(1)} %get-tuple-element.213, ...), kind=kLoop, calls=%fused_computation.28.clone.1 | loop fusion | flops 9172384 | bytes 26112 | tf_op jit(solution)/shard_map/while/body/eval_jaxpr/reduce_sum | solution.py:69
  93.6 3.5 %all-to-all-start.1 = ((f32[16,2,3,544]{3,1,2,0:T(2,128)}), f32[16,2,3,544]{3,1,2,0:T(2,128)S(1)}, u32[]{:S(2)}, u32[]{:S(2)}) async-start(f32[16,2,3,544]{3,1,2,0:T(2,128)} %copy.52), calls=%async_computation.1 | async-start | bytes 491520 | tf_op jit(solution)/shard_map/all_to_all | solution.py:34
  97.0 11.4 %all-to-all-done.1 = f32[16,2,3,544]{3,1,2,0:T(2,128)S(1)} async-done(((f32[16,2,3,544]{3,1,2,0:T(2,128)}), f32[16,2,3,544]{3,1,2,0:T(2,128)S(1)}, u32[]{:S(2)}, u32[]{:S(2)}) %all-to-all-start.1) | async-done | bytes 208928 | tf_op jit(solution)/shard_map/all_to_all | solution.py:34
  109.5 13.8 %all_to_all.25 = f32[16,2,3,544]{3,1,2,0:T(2,128)S(1)} all-to-all(f32[16,2,3,544]{3,1,2,0:T(2,128)S(1)} %broadcast_in_dim.24), channel_id=1, replica_groups=mesh['space'=64,'lane'=16] {'lane'}, dimensions={0} | all-to-all | bytes 417792 | tf_op jit(solution)/shard_map/all_to_all | solution.py:46
  127.8 12.4 %all-to-all-start.3 = ((f32[64,1,3264]{2,1,0:T(1,128)}), f32[64,1,3264]{2,1,0:T(1,128)S(1)}, u32[]{:S(2)}, u32[]{:S(2)}) async-start(f32[64,1,3264]{2,1,0:T(1,128)} %copy.57), calls=%async_computation.3 | async-start | bytes 1703936 | tf_op jit(solution)/shard_map/all_to_all | solution.py:129
  141.4 23.2 %all-to-all-done.3 = f32[64,1,3264]{2,1,0:T(1,128)S(1)} async-done(((f32[64,1,3264]{2,1,0:T(1,128)}), f32[64,1,3264]{2,1,0:T(1,128)S(1)}, u32[]{:S(2)}, u32[]{:S(2)}) %all-to-all-start.3) | async-done | bytes 835616 | tf_op jit(solution)/shard_map/all_to_all | solution.py:129
  164.6 3.1 %reduce.21 = f32[64,3264]{1,0:T(8,128)} reduce(f32[64,1,3264]{2,1,0:T(1,128)S(1)} %all-to-all-done.3, f32[]{:T(128)} %constant.110), dimensions={1}, to_apply=%all_to_all.18.reduce_sub_computation | reduce | bytes 1671172 | tf_op jit(solution)/shard_map/all_to_all | solution.py:129
  171.0 2.8 %slice_bitcast_fusion = (f32[96,3,544]{2,1,0:T(4,128)}, f32[96,3,544]{2,1,0:T(4,128)S(1)}) fusion(f32[96,2,3,544]{3,2,1,0:T(4,128)} %constant_dynamic-update-slice_fusion.1), kind=kLoop, calls=%fused_computation.88 | loop fusion | bytes 2506752 | tf_op jit(solution)/shard_map/squeeze | solution.py:134
  176.8 18.5 %while.21 = (s32[]{:T(128)}, f32[8,3,544]{2,1,0:T(4,128)S(1)}, f32[8,3,544]{2,1,0:T(4,128)S(1)}, f32[8,3,544]{2,1,0:T(4,128)S(1)}, f32[8,3,544]{2,1,0:T(4,128)S(1)}, /*index=5*/s32[]{:T(128)}, s32[]{:T(128)}, s32[]{}, s32[]{}) while((s32[]{:T(128)}, f32[8,3,544]{2,1,0:T(4,128)S(1)}, f32[8,3,544]{2,1,0:T(4,128)S(1)}, ...), condition=%wide.region_12.13_spmd, body=%wide.region_8.12_spmd.sunk | while | flops 9177284 | bytes 96401 | solution.py:90
  176.9 2.1 %fusion.65 = (f32[544]{0:T(1024)S(1)}, f32[544]{0:T(1024)S(1)}, f32[544]{0:T(1024)S(1)}) fusion(f32[544]{0:T(1024)S(1)} %get-tuple-element.226, f32[544]{0:T(1024)S(1)} %get-tuple-element.227, f32[544]{0:T(1024)S(1)} %get-tuple-element.228, f32[544]{0:T(1024)S(1)} %get-tuple-element.229, f32[544]{0:T(1024)S(1)} %get-tuple-element.230, ...), kind=kLoop, calls=%fused_computation.64.clone.1 | loop fusion | flops 9172384 | bytes 26112 | tf_op jit(solution)/shard_map/while/body/eval_jaxpr/reduce_sum | solution.py:69
  179.3 2.1 %fusion.65 = (f32[544]{0:T(1024)S(1)}, f32[544]{0:T(1024)S(1)}, f32[544]{0:T(1024)S(1)}) fusion(f32[544]{0:T(1024)S(1)} %get-tuple-element.226, f32[544]{0:T(1024)S(1)} %get-tuple-element.227, f32[544]{0:T(1024)S(1)} %get-tuple-element.228, f32[544]{0:T(1024)S(1)} %get-tuple-element.229, f32[544]{0:T(1024)S(1)} %get-tuple-element.230, ...), kind=kLoop, calls=%fused_computation.64.clone.1 | loop fusion | flops 9172384 | bytes 26112 | tf_op jit(solution)/shard_map/while/body/eval_jaxpr/reduce_sum | solution.py:69
  181.6 2.1 %fusion.65 = (f32[544]{0:T(1024)S(1)}, f32[544]{0:T(1024)S(1)}, f32[544]{0:T(1024)S(1)}) fusion(f32[544]{0:T(1024)S(1)} %get-tuple-element.226, f32[544]{0:T(1024)S(1)} %get-tuple-element.227, f32[544]{0:T(1024)S(1)} %get-tuple-element.228, f32[544]{0:T(1024)S(1)} %get-tuple-element.229, f32[544]{0:T(1024)S(1)} %get-tuple-element.230, ...), kind=kLoop, calls=%fused_computation.64.clone.1 | loop fusion | flops 9172384 | bytes 26112 | tf_op jit(solution)/shard_map/while/body/eval_jaxpr/reduce_sum | solution.py:69
  183.9 2.1 %fusion.65 = (f32[544]{0:T(1024)S(1)}, f32[544]{0:T(1024)S(1)}, f32[544]{0:T(1024)S(1)}) fusion(f32[544]{0:T(1024)S(1)} %get-tuple-element.226, f32[544]{0:T(1024)S(1)} %get-tuple-element.227, f32[544]{0:T(1024)S(1)} %get-tuple-element.228, f32[544]{0:T(1024)S(1)} %get-tuple-element.229, f32[544]{0:T(1024)S(1)} %get-tuple-element.230, ...), kind=kLoop, calls=%fused_computation.64.clone.1 | loop fusion | flops 9172384 | bytes 26112 | tf_op jit(solution)/shard_map/while/body/eval_jaxpr/reduce_sum | solution.py:69
  193.2 2.1 %fusion.65 = (f32[544]{0:T(1024)S(1)}, f32[544]{0:T(1024)S(1)}, f32[544]{0:T(1024)S(1)}) fusion(f32[544]{0:T(1024)S(1)} %get-tuple-element.226, f32[544]{0:T(1024)S(1)} %get-tuple-element.227, f32[544]{0:T(1024)S(1)} %get-tuple-element.228, f32[544]{0:T(1024)S(1)} %get-tuple-element.229, f32[544]{0:T(1024)S(1)} %get-tuple-element.230, ...), kind=kLoop, calls=%fused_computation.64.clone.1 | loop fusion | flops 9172384 | bytes 26112 | tf_op jit(solution)/shard_map/while/body/eval_jaxpr/reduce_sum | solution.py:69
  196.2 15.9 %all_to_all.26 = f32[16,2,3,544]{3,1,2,0:T(2,128)S(1)} all-to-all(f32[16,2,3,544]{3,1,2,0:T(2,128)S(1)} %copy.60), channel_id=1, replica_groups=mesh['space'=64,'lane'=16] {'lane'}, dimensions={0} | all-to-all | bytes 417792 | tf_op jit(solution)/shard_map/all_to_all | solution.py:34
  (183 shorter events, 51.3 us)
Async XLA Ops:
  0.6 1.4 copy-start
  0.6 3.4 %copy-start.1 = (f32[32,3,544]{2,0,1:T(8,128)S(1)}, f32[32,3,544]{2,0,1:T(8,128)}, u32[]{:S(2)}) copy-start(f32[32,3,544]{2,0,1:T(8,128)} %param.10) | copy-start | bytes 626692
  4.0 0.7 copy-start.5
  5.6 16.5 %copy-start.3 = (s32[1,12]{1,0:T(1,128)S(1)}, s32[1,12]{1,0:T(1,128)}, u32[]{:S(2)}) copy-start(s32[1,12]{1,0:T(1,128)} %param.14) | copy-start | bytes 148
  5.6 16.5 %copy-start.4 = (s32[1,12]{1,0:T(1,128)S(1)}, s32[1,12]{1,0:T(1,128)}, u32[]{:S(2)}) copy-start(s32[1,12]{1,0:T(1,128)} %param.13) | copy-start | bytes 148
  7.4 56.0 %all-to-all-start = ((f32[64,1,3264]{2,1,0:T(1,128)}), f32[64,1,3264]{2,1,0:T(1,128)S(1)}, u32[]{:S(2)}, u32[]{:S(2)}) async-start(f32[64,1,3264]{2,1,0:T(1,128)} %copy.49), calls=%async_computation | async-start | bytes 1703936 | tf_op jit(solution)/shard_map/all_to_all | solution.py:129
  93.6 14.9 %all-to-all-start.1 = ((f32[16,2,3,544]{3,1,2,0:T(2,128)}), f32[16,2,3,544]{3,1,2,0:T(2,128)S(1)}, u32[]{:S(2)}, u32[]{:S(2)}) async-start(f32[16,2,3,544]{3,1,2,0:T(2,128)} %copy.52), calls=%async_computation.1 | async-start | bytes 491520 | tf_op jit(solution)/shard_map/all_to_all | solution.py:34
  127.8 36.8 %all-to-all-start.3 = ((f32[64,1,3264]{2,1,0:T(1,128)}), f32[64,1,3264]{2,1,0:T(1,128)S(1)}, u32[]{:S(2)}, u32[]{:S(2)}) async-start(f32[64,1,3264]{2,1,0:T(1,128)} %copy.57), calls=%async_computation.3 | async-start | bytes 1703936 | tf_op jit(solution)/shard_map/all_to_all | solution.py:129
  212.2 0.6 copy-start.2
where the time goes:
time: 214 us; the launch traced here: 213 us
  blocking collectives  60.2 us (28%)
  other arithmetic  46.7 us (22%)
  waiting for transfers between devices  34.6 us (16%)
  local copies, waits for them, and re-layouts  34.1 us (16%)
  starting transfers between devices  29.9 us (14%)
  matrix products  3.89 us (2%)
  between operations  2.38 us (1%)
    reduce_sum x16, other arithmetic, stokes_tile(): jnp.sum(weight_direct * source_force[0][None, :] + weight_tensor * off_x,...  34.1 us
    all_gather x1, blocking collectives, sent_together(): out = lax.all_gather(both, axis, axis=dim, tiled=True)  30.5 us
    all_to_all x2, starting transfers between devices, shards(): lax.all_to_all(outgoing, 'space', split_axis=0, concat_axis=0, tiled=True)  26.4 us
    all_to_all x2, waiting for transfers between devices, shards(): lax.all_to_all(outgoing, 'space', split_axis=0, concat_axis=0, tiled=True)  23.2 us
    all_to_all x1, blocking collectives, sum_at_owner(): lax.all_to_all(blocks, axis, split_axis=0, concat_axis=0, tiled=True)  15.9 us
    all_to_all x1, blocking collectives, copy_for_each(): lax.all_to_all(jnp.broadcast_to(value[None], (peers, *value.shape)), axis...  13.8 us
    all_to_all x1, waiting for transfers between devices, sum_at_owner(): lax.all_to_all(blocks, axis, split_axis=0, concat_axis=0, tiled=True)  11.4 us
    concatenate x4, local copies, waits for them, and re-layouts, shards(): jnp.concatenate([packed, incoming.reshape(-1, 6 * points)], axis=0)  6.53 us
  transfers between devices with their start and end apart: 3, of which 2 were waited for; matrix products, arithmetic and copies ran while one was open for 5% of the time, Pallas kernels for 0%

commit v1 on v0

v1 whole, which is shorter than its diff:
```python
import functools
import math

import jax
import jax.numpy as jnp
from jax import lax
from jax.experimental import pallas as pl
from jax.experimental.pallas import tpu as pltpu
from jax.sharding import PartitionSpec as P

ITERS = 2
MESH = pl.DeviceIdType.MESH
ROW = 128


def ring_offsets(side):
    def hops(d):
        return min(d, side - d)

    every = [(dy, dx) for dy in range(side) for dx in range(side)]
    return sorted(every, key=lambda o: (hops(o[0]) + hops(o[1]), o))


def split_bf16(value):
    high = value.astype(jnp.bfloat16)
    return high, (value - high.astype(jnp.float32)).astype(jnp.bfloat16)


def kernel(
    cfg,
    own_ref,
    bend_ref,
    send_ref,
    target_ref,
    source_ref,
    count_ref,
    moved_ref,
    vel_ref,
    pool,
    force,
    bend_hi,
    bend_lo,
    out_box,
    ghost_box,
    broad,
    result,
    own_slice,
    move_out,
    move_in,
    last_out,
    last_in,
    task_out,
    task_in,
    picks_v,
    picks_s,
    send_a,
    recv_a,
    relay_a,
    send_c,
    recv_c,
    relay_c,
    send_d,
    recv_d,
    send_t,
    recv_t,
    local_sem,
):
    owners, lanes, cells, points, cap, slots = cfg
    side = math.isqrt(owners)
    half = owners // 2
    planes = lanes // 2
    pool_cells = cells + owners
    width = own_ref.shape[1]
    chunks = width // ROW
    piece = points // lanes
    rows_piece = -(-piece // 8) * 8
    groups = rows_piece // 8
    cell_rows = 3 * rows_piece
    share = cells // lanes
    box_rows = -(-3 * chunks // 8) * 8
    f32 = jnp.float32

    space = lax.axis_index("space")
    lane = lax.axis_index("lane")
    core = lax.rem(lane, 2)
    plane = lane // 2
    partner = lane + 1 - 2 * core
    y, x = space // side, lax.rem(space, side)
    offsets = ring_offsets(side)

    def owner_at(j, which, sign):
        (ay, ax), (by, bx) = offsets[2 * j], offsets[2 * j + 1]
        dy = jnp.where(which == 0, ay, by)
        dx = jnp.where(which == 0, ax, bx)
        ny = lax.rem(y + sign * dy + side, side)
        nx = lax.rem(x + sign * dx + side, side)
        return ny * side + nx

    def unless_self(j, which, act):
        if j == 0:
            pl.when(which == 1)(act)
        else:
            act()

    barrier = pltpu.get_barrier_semaphore()
    for j in range(half):

        def greet(j=j):
            pl.semaphore_signal(
                barrier, inc=1, device_id=(owner_at(j, core, -1), lane), device_id_type=MESH
            )

        unless_self(j, core, greet)
    for o in range(1, lanes):
        pl.semaphore_signal(
            barrier, inc=1, device_id=(space, lax.rem(lane + o, lanes)), device_id_type=MESH
        )

    task_out[...] = jnp.zeros_like(task_out)
    task_out[0:1, 0:cap] = target_ref[...]
    task_out[1:2, 0:cap] = source_ref[...]
    task_out[2:3, 0:1] = count_ref[...]
    task_in[pl.ds(pl.multiple_of(8 * lane, 8), 8), :] = task_out[...]
    for c in range(3):
        pool[0, c * pool_cells : c * pool_cells + cells, :] = own_ref[c * cells : (c + 1) * cells, :]
    bend_hi[...] = jnp.zeros_like(bend_hi)
    bend_lo[...] = jnp.zeros_like(bend_lo)
    high, low = split_bf16(bend_ref[...])
    bend_hi[0:points, 0:points] = high
    bend_lo[0:points, 0:points] = low
    result[...] = jnp.zeros_like(result)

    def stage_ghosts(step):
        for j in range(half):

            def stage(j=j):
                cell = send_ref[0, owner_at(j, core, 1)]
                for c in range(3):
                    row = pool[step, pl.ds(c * pool_cells + cell, 1), :]
                    for k in range(chunks):
                        at = box_rows * j + c * chunks + k
                        out_box[step, at : at + 1, :] = row[:, k * ROW : (k + 1) * ROW]

            unless_self(j, core, stage)

    def ghost_copy(step, j):
        return pltpu.make_async_remote_copy(
            src_ref=out_box.at[step, pl.ds(box_rows * j, box_rows), :],
            dst_ref=ghost_box.at[step, pl.ds(pl.multiple_of(box_rows * space, 8), box_rows), :],
            send_sem=send_a.at[step, j],
            recv_sem=recv_a.at[step, space],
            device_id=(owner_at(j, core, 1), lane),
            device_id_type=MESH,
        )

    def ghost_pass(step, j, which):
        origin = owner_at(j, which, -1)
        at = pl.ds(pl.multiple_of(box_rows * origin, 8), box_rows)
        return pltpu.make_async_remote_copy(
            src_ref=ghost_box.at[step, at, :],
            dst_ref=ghost_box.at[step, at, :],
            send_sem=relay_a.at[step, j],
            recv_sem=recv_a.at[step, origin],
            device_id=(space, partner),
            device_id_type=MESH,
        )

    def exchange_ghosts(step):
        for j in range(half):
            unless_self(j, core, lambda j=j: ghost_copy(step, j).start())

    def collect_ghosts(step):
        for j in range(half):

            def take(j=j):
                ghost_pass(step, j, core).wait_recv()
                ghost_pass(step, j, core).start()

            unless_self(j, core, take)
        for j in range(half):
            unless_self(j, 1 - core, lambda j=j: ghost_pass(step, j, 1 - core).wait_recv())
        cell = send_ref[0, space]
        for c in range(3):
            row = pool[step, pl.ds(c * pool_cells + cell, 1), :]
            for k in range(chunks):
                at = box_rows * space + c * chunks + k
                ghost_box[step, pl.ds(at, 1), :] = row[:, k * ROW : (k + 1) * ROW]
        for c in range(3):
            for d in range(0, owners, 8):
                rows = min(8, owners - d)
                for k in range(chunks):
                    at = c * pool_cells + cells + d
                    pool[step, at : at + rows, k * ROW : (k + 1) * ROW] = ghost_box[
                        step, pl.ds(box_rows * d + c * chunks + k, rows, stride=box_rows), :
                    ]

    def drain_ghosts(step):
        for j in range(half):

            def drain(j=j):
                ghost_copy(step, j).wait_send()
                ghost_pass(step, j, core).wait_send()

            unless_self(j, core, drain)

    def bend(step, first, count):
        for c in range(3):
            at = pl.ds(c * pool_cells + first, count)
            high, low = split_bf16(pool[step, at, :])
            total = jnp.dot(high, bend_hi[...], preferred_element_type=f32)
            total += jnp.dot(low, bend_hi[...], preferred_element_type=f32)
            total += jnp.dot(high, bend_lo[...], preferred_element_type=f32)
            force[at, :] = total

    def spread_targets():
        block = own_slice[...]
        turned = jnp.concatenate(
            [block, jnp.zeros((ROW - cells, ROW), f32)], axis=0
        ).T
        for t in range(cells):
            broad[t] = jnp.broadcast_to(
                turned[0:cell_rows, t : t + 1], (cell_rows, ROW)
            )

    lane_at = lax.broadcasted_iota(jnp.int32, (8, ROW), 1)

    def one_slot(step, slot):
        target = picks_s[0, slot]
        source = picks_s[1, slot]
        there = [
            jnp.broadcast_to(pool[step, pl.ds(c * pool_cells + source, 1), :], (8, width))
            for c in range(3)
        ]
        push = [
            jnp.broadcast_to(force[pl.ds(c * pool_cells + source, 1), :], (8, width))
            for c in range(3)
        ]
        for g in range(groups):
            here = [
                broad[target, c * rows_piece + 8 * g : c * rows_piece + 8 * g + 8, :]
                for c in range(3)
            ]
            off = [
                jnp.concatenate([h] * chunks, axis=1) - p for h, p in zip(here, there)
            ]
            inverse = lax.rsqrt(off[0] * off[0] + off[1] * off[1] + (off[2] * off[2] + 1.0))
            cube = inverse * inverse * inverse
            along = off[0] * push[0] + off[1] * push[1] + off[2] * push[2]
            direct = inverse + cube
            tensor = along * cube
            for c in range(3):
                total = jnp.sum(direct * push[c] + tensor * off[c], axis=1, keepdims=True)
                at = c * rows_piece + 8 * g
                result[at : at + 8, :] = jnp.where(lane_at == slot, total, result[at : at + 8, :])

    def run_tasks(step):
        unroll = next(u for u in (3, 2, 1) if slots % u == 0)

        @pl.loop(0, slots // unroll)
        def _(n):
            for u in range(unroll):
                one_slot(step, n * unroll + u)

    def read_tasks():
        targets = task_in[pl.ds(0, lanes, stride=8), :]
        sources = task_in[pl.ds(1, lanes, stride=8), :]
        counts = jnp.broadcast_to(task_in[pl.ds(2, lanes, stride=8), 0:1], (lanes, ROW))
        row_at = lax.broadcasted_iota(jnp.int32, (lanes, ROW), 0)
        start = jnp.zeros((lanes, ROW), jnp.int32)
        for n in range(lanes - 1):
            start += jnp.where(row_at > n, counts[n : n + 1, :], 0)
        number = lax.broadcasted_iota(jnp.int32, (lanes, ROW), 1) - start
        target = jnp.zeros((lanes, ROW), jnp.int32)
        source = jnp.zeros((lanes, ROW), jnp.int32)
        for j in range(cap):
            hit = (number == j) & (counts > j)
            target += jnp.where(hit, targets[:, j : j + 1], 0)
            source += jnp.where(hit, sources[:, j : j + 1], 0)
        live = (lax.broadcasted_iota(jnp.int32, (1, ROW), 1) < jnp.sum(counts, axis=0, keepdims=True))
        target = jnp.sum(target, axis=0, keepdims=True)
        source = jnp.sum(source, axis=0, keepdims=True)
        picks_v[...] = jnp.zeros_like(picks_v)
        picks_v[0:1, :] = target
        picks_v[1:2, :] = source
        picks_v[2:3, :] = live.astype(jnp.int32)
        copy = pltpu.make_async_copy(picks_v, picks_s, local_sem)
        copy.start()
        copy.wait()

    def velocities():
        match = (
            (lax.broadcasted_iota(jnp.int32, (cells, ROW), 0) == picks_v[0:1, :])
            & (picks_v[2:3, :] > 0)
        ).astype(f32)
        total = lax.dot_general(
            match,
            result[...],
            (((1,), (1,)), ((), ())),
            precision=lax.Precision.HIGHEST,
            preferred_element_type=f32,
        )
        return total * (1.0 / points)

    def assemble(blocks, rows):
        at = lax.broadcasted_iota(jnp.int32, (rows, ROW), 1)
        whole = [[jnp.zeros((rows, ROW), f32) for _ in range(chunks)] for _ in range(3)]
        for n in range(lanes):
            for c in range(3):
                first = piece * n
                shift = (first - c * rows_piece) % ROW
                block = blocks[n] if shift == 0 else pltpu.roll(blocks[n], shift, 1)
                k, low = divmod(first, ROW)
                high = low + piece
                whole[c][k] = jnp.where((at >= low) & (at < high), block, whole[c][k])
                if high > ROW:
                    whole[c][k + 1] = jnp.where(at < high - ROW, block, whole[c][k + 1])
        return whole

    def lane_copies(source_at, inbox, rows, send, recv):
        made = []
        for o in range(1, lanes):
            other = lax.rem(lane + o, lanes)
            made.append(
                pltpu.make_async_remote_copy(
                    src_ref=source_at(other),
                    dst_ref=inbox.at[pl.ds(pl.multiple_of(rows * lane, 8), rows), :],
                    send_sem=send.at[o],
                    recv_sem=recv.at[o],
                    device_id=(space, other),
                    device_id_type=MESH,
                )
            )
        return made

    lane_of = lax.broadcasted_iota(jnp.int32, (width, ROW), 1)
    point_of = lax.broadcasted_iota(jnp.int32, (width, ROW), 0) - piece * lane
    mine = jnp.zeros((cells, ROW), f32)
    for c in range(3):
        pick = (point_of == lane_of - c * rows_piece) & (point_of >= 0) & (point_of < piece)
        mine += jnp.dot(
            pool[0, c * pool_cells : c * pool_cells + cells, :],
            pick.astype(f32),
            precision=lax.Precision.HIGHEST,
            preferred_element_type=f32,
        )
    own_slice[...] = mine
    spread_targets()
    stage_ghosts(0)

    for core_is in range(2):
        pl.when(core == core_is)(
            lambda n=half - 1 + core_is + lanes - 1: pl.semaphore_wait(barrier, n)
        )

    task_copies = lane_copies(lambda other: task_out, task_in, 8, send_t, recv_t)
    for copy in task_copies:
        copy.start()
    exchange_ghosts(0)
    bend(0, 0, cells)
    for copy in task_copies:
        copy.wait()
    read_tasks()
    collect_ghosts(0)
    bend(0, cells, owners)
    run_tasks(0)
    drain_ghosts(0)

    own_slice[...] += velocities()
    move_out[...] = own_slice[...]

    def move_copy(o):
        return pltpu.make_async_remote_copy(
            src_ref=move_out,
            dst_ref=move_in.at[pl.ds(pl.multiple_of(cells * lane, 8), cells), :],
            send_sem=send_c.at[o],
            recv_sem=recv_c.at[lane],
            device_id=(space, 2 * lax.rem(plane + o, planes) + core),
            device_id_type=MESH,
        )

    def move_pass(o, which):
        origin = 2 * lax.rem(plane + planes - o, planes) + which
        at = pl.ds(pl.multiple_of(cells * origin, 8), cells)
        return pltpu.make_async_remote_copy(
            src_ref=move_out if o == 0 else move_in.at[at, :],
            dst_ref=move_in.at[at, :],
            send_sem=relay_c.at[o],
            recv_sem=recv_c.at[origin],
            device_id=(space, partner),
            device_id_type=MESH,
        )

    near_first = sorted(range(1, planes), key=lambda o: min(o, planes - o))
    for o in near_first:
        move_copy(o).start()
    move_pass(0, core).start()
    move_in[pl.ds(pl.multiple_of(cells * lane, 8), cells), :] = own_slice[...]
    spread_targets()
    for o in near_first:
        move_pass(o, core).wait_recv()
        move_pass(o, core).start()
    for o in range(planes):
        move_pass(o, 1 - core).wait_recv()
    whole = assemble([move_in[cells * n : cells * (n + 1), :] for n in range(lanes)], cells)
    for c in range(3):
        for k in range(chunks):
            at = c * pool_cells
            pool[1, at : at + cells, k * ROW : (k + 1) * ROW] = whole[c][k]

    stage_ghosts(1)
    exchange_ghosts(1)
    bend(1, 0, cells)
    for o in near_first:
        move_copy(o).wait_send()
    for o in range(planes):
        move_pass(o, core).wait_send()
    collect_ghosts(1)
    bend(1, cells, owners)
    run_tasks(1)
    drain_ghosts(1)

    speed = velocities()
    last_out[...] = jnp.zeros_like(last_out)
    for n in range(lanes):
        last_out[8 * n : 8 * n + share, :] = speed[n * share : (n + 1) * share, :]
    last_copies = lane_copies(
        lambda other: last_out.at[pl.ds(pl.multiple_of(8 * other, 8), 8), :],
        last_in,
        8,
        send_d,
        recv_d,
    )
    for copy in last_copies:
        copy.start()
    here = pl.ds(pl.multiple_of(8 * lane, 8), 8)
    last_in[here, :] = last_out[here, :]
    for copy in last_copies:
        copy.wait()
    whole = assemble([last_in[8 * n : 8 * (n + 1), :] for n in range(lanes)], 8)
    for c in range(3):
        speeds = jnp.concatenate(whole[c], axis=1)
        for n in range(share):
            cell = pool[1, pl.ds(c * pool_cells + share * lane + n, 1), :]
            vel_ref[n, c : c + 1, :] = speeds[n : n + 1, 0:points]
            moved_ref[n, c : c + 1, :] = (0.5 * (cell + speeds[n : n + 1, :]))[:, 0:points]


def shards(owners, lanes, positions, bend_op, send_list, task_target, task_source, task_count):
    cells, _, points = positions.shape
    cap = task_target.shape[1]
    slots = cap + 7 * (lanes - 1)
    width = -(-points // ROW) * ROW
    chunks = width // ROW
    piece = points // lanes
    rows_piece = -(-piece // 8) * 8
    cell_rows = 3 * rows_piece
    box_rows = -(-3 * chunks // 8) * 8
    share = cells // lanes
    pool_cells = cells + owners
    half = owners // 2
    planes = lanes // 2
    f32 = jnp.float32
    own = jnp.pad(
        2.0 * jnp.transpose(positions, (1, 0, 2)), ((0, 0), (0, 0), (0, width - points))
    ).reshape(3 * cells, width)
    vmem = pl.BlockSpec(memory_space=pltpu.VMEM)
    smem = pl.BlockSpec(memory_space=pltpu.SMEM)
    dma = pltpu.SemaphoreType.DMA
    out = jax.ShapeDtypeStruct((share, 3, points), f32)
    return pl.pallas_call(
        functools.partial(kernel, (owners, lanes, cells, points, cap, slots)),
        out_shape=(out, out),
        in_specs=[vmem, vmem, smem, vmem, vmem, vmem],
        out_specs=(vmem, vmem),
        scratch_shapes=[
            pltpu.VMEM((ITERS, 3 * pool_cells, width), f32),
            pltpu.VMEM((3 * pool_cells, width), f32),
            pltpu.VMEM((width, width), jnp.bfloat16),
            pltpu.VMEM((width, width), jnp.bfloat16),
            pltpu.VMEM((ITERS, half * box_rows, ROW), f32),
            pltpu.VMEM((ITERS, owners * box_rows, ROW), f32),
            pltpu.VMEM((cells, cell_rows, ROW), f32),
            pltpu.VMEM((ROW, ROW), f32),
            pltpu.VMEM((cells, ROW), f32),
            pltpu.VMEM((cells, ROW), f32),
            pltpu.VMEM((lanes * cells, ROW), f32),
            pltpu.VMEM((lanes * 8, ROW), f32),
            pltpu.VMEM((lanes * 8, ROW), f32),
            pltpu.VMEM((8, ROW), jnp.int32),
            pltpu.VMEM((lanes * 8, ROW), jnp.int32),
            pltpu.VMEM((8, ROW), jnp.int32),
            pltpu.SMEM((8, ROW), jnp.int32),
            dma((ITERS, half)),
            dma((ITERS, owners)),
            dma((ITERS, half)),
            dma((planes,)),
            dma((lanes,)),
            dma((planes,)),
            dma((lanes,)),
            dma((lanes,)),
            dma((lanes,)),
            dma((lanes,)),
            dma,
        ],
        compiler_params=pltpu.CompilerParams(
            collective_id=0, has_side_effects=True, vmem_limit_bytes=48 * 1024 * 1024
        ),
    )(own, bend_op, send_list, task_target, task_source, task_count.reshape(1, 1))


def solution(mesh):
    owners, lanes = mesh.shape["space"], mesh.shape["lane"]
    in_specs = (
        P("space", None, None),
        P(),
        P("space", None),
        P(("space", "lane"), None),
        P(("space", "lane"), None),
        P(("space", "lane")),
    )
    out_specs = (P(("space", "lane"), None, None), P(("space", "lane"), None, None))
    return jax.shard_map(
        functools.partial(shards, owners, lanes),
        mesh=mesh,
        in_specs=in_specs,
        out_specs=out_specs,
        check_vma=False,
    )
```

time: 214 us -> 107 us (0.50)
  Pallas kernels: 0 us -> 99.8 us
  blocking collectives: 60.2 us -> 0 us
  other arithmetic: 46.7 us -> 0.96 us
  waiting for transfers between devices: 34.6 us -> 0 us
  starting transfers between devices: 29.9 us -> 0 us
  local copies, waits for them, and re-layouts: 34.1 us -> 4.54 us
  matrix products: 3.89 us -> 0 us
    pallas_call x0 -> x1, Pallas kernels: none -> 99.8 us  [shards(): pl.pallas_call(functools.partial(kernel, (owners, lanes, cells, points, c...]
    reduce_sum x19 -> x0, other arithmetic: 35 us -> none  [the longest x16 34.1 us: stokes_tile(): jnp.sum(weight_direct * source_force[0][None, :] + weight_tensor * off_x,...]
    all_to_all x3 -> x0, waiting for transfers between devices: 34.6 us -> none  [the longest x2 23.2 us: shards(): lax.all_to_all(outgoing, 'space', split_axis=0, concat_axis=0, tiled=True)]
    all_gather x1 -> x0, blocking collectives: 30.5 us -> none  [sent_together(): out = lax.all_gather(both, axis, axis=dim, tiled=True)]
    all_to_all x3 -> x0, starting transfers between devices: 29.9 us -> none  [the longest x2 26.4 us: shards(): lax.all_to_all(outgoing, 'space', split_axis=0, concat_axis=0, tiled=True)]
    all_to_all x2 -> x0, blocking collectives: 29.7 us -> none  [the longest x1 15.9 us: sum_at_owner(): lax.all_to_all(blocks, axis, split_axis=0, concat_axis=0, tiled=True)]
    gather x12 -> x0, local copies, waits for them, and re-layouts: 11.1 us -> none  [the longest x2 2.4 us: tile_batch(): force_rows = pool_frc[slot_sources]]
    concatenate x6 -> x0, local copies, waits for them, and re-layouts: 7.13 us -> none  [the longest x4 6.53 us: shards(): jnp.concatenate([packed, incoming.reshape(-1, 6 * points)], axis=0)]
  transfers between devices with their start and end apart: 3 -> 0, of which waited for: 2 -> 0; matrix products, arithmetic and copies ran while one was open for 5% -> 0% of each run, Pallas kernels for 0% -> 0%
where the time goes in v1:
time: 107 us
  Pallas kernels  99.8 us (93%)
  local copies, waits for them, and re-layouts  4.54 us (4%)
  between operations  1.31 us (1%)
    pallas_call x1, Pallas kernels, shards(): pl.pallas_call(functools.partial(kernel, (owners, lanes, cells, points, c...  99.8 us
    unnamed x8, local copies, waits for them, and re-layouts  3.3 us

profile of v1, /device:TPU:1, one launch (start us, length us, event | category | flops | bytes accessed | tf_op | source)
XLA Modules:
  0.0 106.6 jit_solution(10421154701608297766)
XLA Ops:
  0.6 1.0 multiply_bitcast_fusion
  2.3 0.0 copy-start
  2.3 1.3 %copy-done = f32[544,544]{1,0:T(8,128)S(1)} copy-done((f32[544,544]{1,0:T(8,128)S(1)}, f32[544,544]{1,0:T(8,128)}, u32[]{:S(2)}) %copy-start) | copy-done | bytes 1183768
  3.6 0.0 copy-start.1
  3.6 0.7 copy-done.1
  4.3 0.0 copy-start.2
  4.3 0.7 copy-done.2
  4.9 0.0 copy-start.3
  4.9 0.7 copy-done.3
  5.6 99.8 %shard_map.77 = (f32[2,3,544]{2,1,0:T(4,128)S(1)}, f32[2,3,544]{2,1,0:T(4,128)S(1)}) custom-call(f32[96,640]{1,0:T(8,128)S(1)} %bitcast.5, f32[544,544]{1,0:T(8,128)S(1)} %copy-done, s32[1,64]{1,0:T(1,128)S(1)} %copy-done.1, s32[1,12]{1,0:T(1,128)S(1)} %copy-done.2, s32[1,12]{1,0:T(1,128)S(1)} %copy-done.3, s32[1,1]{1,0:T(1,128)} %bitcast.4.count_ref), custom_call_target="tpu_custom_call" | custom-call | tf_op jit(solution)/shard_map/pallas_call | solution.py:470
  105.4 0.6 copy.8
  106.0 0.6 copy.9
  (1 shorter events, 0.0 us)
Async XLA Ops:
  2.3 1.3 %copy-start = (f32[544,544]{1,0:T(8,128)S(1)}, f32[544,544]{1,0:T(8,128)}, u32[]{:S(2)}) copy-start(f32[544,544]{1,0:T(8,128)} %bend_ref.1) | copy-start | bytes 3551236
  3.6 0.7 copy-start.1
  4.3 0.7 copy-start.2
  4.9 0.7 copy-start.3

commit v2 on v1

--- a/solution.py
+++ b/solution.py
@@ -11,6 +11,7 @@
 ITERS = 2
 MESH = pl.DeviceIdType.MESH
 ROW = 128
+SEGMENT = 32
 
 
 def ring_offsets(side):
@@ -28,12 +29,12 @@
 
 def kernel(
     cfg,
-    own_ref,
-    bend_ref,
-    send_ref,
-    target_ref,
-    source_ref,
-    count_ref,
+    own_hbm,
+    bend_hbm,
+    send_hbm,
+    target_hbm,
+    source_hbm,
+    count_hbm,
     moved_ref,
     vel_ref,
     pool,
@@ -64,17 +65,28 @@
     send_t,
     recv_t,
     local_sem,
+    own_ref,
+    bend_ref,
+    send_ref,
+    target_ref,
+    source_ref,
+    count_ref,
+    load_sem,
+    result_tail,
 ):
     owners, lanes, cells, points, cap, slots = cfg
     side = math.isqrt(owners)
     half = owners // 2
     planes = lanes // 2
     pool_cells = cells + owners
-    width = own_ref.shape[1]
+    width = pool.shape[2]
     chunks = width // ROW
+    full = points // ROW
     piece = points // lanes
     rows_piece = -(-piece // 8) * 8
-    groups = rows_piece // 8
+    groups = piece // 8
+    assert chunks == full + 1 and points % ROW <= SEGMENT and groups == 4 and piece % 8 == 2
+    quads = -(-slots // 4)
     cell_rows = 3 * rows_piece
     share = cells // lanes
     box_rows = -(-3 * chunks // 8) * 8
@@ -116,19 +128,47 @@
             barrier, inc=1, device_id=(space, lax.rem(lane + o, lanes)), device_id_type=MESH
         )
 
+    loads = [
+        pltpu.make_async_copy(src, dst, load_sem.at[n])
+        for n, (src, dst) in enumerate(
+            (
+                (target_hbm, target_ref),
+                (source_hbm, source_ref),
+                (count_hbm, count_ref),
+                (own_hbm, own_ref),
+                (send_hbm, send_ref),
+                (bend_hbm, bend_ref),
+            )
+        )
+    ]
+    for load in loads:
+        load.start()
+
+    def tail(value):
+        rest = value[:, full * ROW : points]
+        if rest.shape[1] < SEGMENT:
+            rest = jnp.concatenate(
+                [rest, jnp.zeros((rest.shape[0], SEGMENT - rest.shape[1]), rest.dtype)], axis=1
+            )
+        return jnp.concatenate([rest] * (ROW // SEGMENT), axis=1)
+
+    result[...] = jnp.zeros_like(result)
+    bend_hi[points:, :] = jnp.zeros((width - points, width), jnp.bfloat16)
+    bend_lo[points:, :] = jnp.zeros((width - points, width), jnp.bfloat16)
+    for load in loads[:3]:
+        load.wait()
     task_out[...] = jnp.zeros_like(task_out)
     task_out[0:1, 0:cap] = target_ref[...]
     task_out[1:2, 0:cap] = source_ref[...]
     task_out[2:3, 0:1] = count_ref[...]
     task_in[pl.ds(pl.multiple_of(8 * lane, 8), 8), :] = task_out[...]
+    loads[3].wait()
     for c in range(3):
-        pool[0, c * pool_cells : c * pool_cells + cells, :] = own_ref[c * cells : (c + 1) * cells, :]
-    bend_hi[...] = jnp.zeros_like(bend_hi)
-    bend_lo[...] = jnp.zeros_like(bend_lo)
-    high, low = split_bf16(bend_ref[...])
-    bend_hi[0:points, 0:points] = high
-    bend_lo[0:points, 0:points] = low
-    result[...] = jnp.zeros_like(result)
+        at = c * pool_cells
+        value = 2.0 * own_ref[:, c, :]
+        pool[0, at : at + cells, 0 : full * ROW] = value[:, 0 : full * ROW]
+        pool[0, at : at + cells, full * ROW :] = tail(value)
+    loads[4].wait()
 
     def stage_ghosts(step):
         for j in range(half):
@@ -212,54 +252,116 @@
             total += jnp.dot(high, bend_lo[...], preferred_element_type=f32)
             force[at, :] = total
 
+    lane_at = lax.broadcasted_iota(jnp.int32, (8, ROW), 1)
+    row_pair = lax.broadcasted_iota(jnp.int32, (8, ROW), 0) // 2
+
     def spread_targets():
         block = own_slice[...]
         turned = jnp.concatenate(
             [block, jnp.zeros((ROW - cells, ROW), f32)], axis=0
         ).T
         for t in range(cells):
-            broad[t] = jnp.broadcast_to(
-                turned[0:cell_rows, t : t + 1], (cell_rows, ROW)
-            )
-
-    lane_at = lax.broadcasted_iota(jnp.int32, (8, ROW), 1)
-
-    def one_slot(step, slot):
-        target = picks_s[0, slot]
-        source = picks_s[1, slot]
-        there = [
-            jnp.broadcast_to(pool[step, pl.ds(c * pool_cells + source, 1), :], (8, width))
-            for c in range(3)
-        ]
-        push = [
-            jnp.broadcast_to(force[pl.ds(c * pool_cells + source, 1), :], (8, width))
-            for c in range(3)
-        ]
-        for g in range(groups):
-            here = [
-                broad[target, c * rows_piece + 8 * g : c * rows_piece + 8 * g + 8, :]
+            block = jnp.broadcast_to(turned[0:cell_rows, t : t + 1], (cell_rows, ROW))
+            broad[t, 0:cell_rows, :] = block
+            for c in range(3):
+                mixed = block[c * rows_piece : c * rows_piece + 8]
+                for g in range(1, groups):
+                    at = c * rows_piece + 8 * g
+                    mixed = jnp.where(lane_at >= SEGMENT * g, block[at : at + 8], mixed)
+                broad[t, cell_rows + 8 * c : cell_rows + 8 * c + 8, :] = mixed
+
+    def terms(here, there, push):
+        off = [h - p for h, p in zip(here, there)]
+        inverse = lax.rsqrt(off[0] * off[0] + off[1] * off[1] + (off[2] * off[2] + 1.0))
+        cube = inverse * inverse * inverse
+        along = off[0] * push[0] + off[1] * push[1] + off[2] * push[2]
+        direct = inverse + cube
+        tensor = along * cube
+        return [direct * f + tensor * o for f, o in zip(push, off)]
+
+    def wide(block, times):
+        return jnp.concatenate([block] * times, axis=1)
+
+    def folded(value):
+        total = value[:, 0:ROW]
+        for k in range(1, value.shape[1] // ROW):
+            total += value[:, k * ROW : (k + 1) * ROW]
+        return total
+
+    def place(box, at, lane_here, value):
+        total = jnp.sum(value, axis=1, keepdims=True)
+        box[at : at + 8, :] = jnp.where(lane_at == lane_here, total, box[at : at + 8, :])
+
+    def four_slots(step, n):
+        last_here = last_there = last_push = None
+        for j in range(4):
+            slot = n + quads * j
+            target = picks_s[0, slot]
+            source = picks_s[1, slot]
+            there = [
+                jnp.broadcast_to(pool[step, pl.ds(c * pool_cells + source, 1), :], (8, width))
                 for c in range(3)
             ]
-            off = [
-                jnp.concatenate([h] * chunks, axis=1) - p for h, p in zip(here, there)
+            push = [
+                jnp.broadcast_to(force[pl.ds(c * pool_cells + source, 1), :], (8, width))
+                for c in range(3)
             ]
-            inverse = lax.rsqrt(off[0] * off[0] + off[1] * off[1] + (off[2] * off[2] + 1.0))
-            cube = inverse * inverse * inverse
-            along = off[0] * push[0] + off[1] * push[1] + off[2] * push[2]
-            direct = inverse + cube
-            tensor = along * cube
-            for c in range(3):
-                total = jnp.sum(direct * push[c] + tensor * off[c], axis=1, keepdims=True)
-                at = c * rows_piece + 8 * g
-                result[at : at + 8, :] = jnp.where(lane_at == slot, total, result[at : at + 8, :])
+            mixed = terms(
+                [broad[target, cell_rows + 8 * c : cell_rows + 8 * c + 8, :] for c in range(3)],
+                [p[:, full * ROW :] for p in there],
+                [p[:, full * ROW :] for p in push],
+            )
+            for g in range(groups):
+                rows = [c * rows_piece + 8 * g for c in range(3)]
+                here = [wide(broad[target, r : r + 8, :], full) for r in rows]
+                whole = terms(
+                    here, [p[:, : full * ROW] for p in there], [p[:, : full * ROW] for p in push]
+                )
+                part = (lane_at >= SEGMENT * g) & (lane_at < SEGMENT * (g + 1))
+                for c in range(3):
+                    place(result, rows[c], slot, folded(whole[c]) + jnp.where(part, mixed[c], 0.0))
+            rows = [c * rows_piece + 8 * groups for c in range(3)]
+            here = [broad[target, r : r + 8, :] for r in rows]
+            if j == 0:
+                last_here, last_there, last_push = here, there, push
+            else:
+                own = row_pair == j
+                own_wide = wide(own, chunks)
+                last_here = [jnp.where(own, a, b) for a, b in zip(here, last_here)]
+                last_there = [jnp.where(own_wide, a, b) for a, b in zip(there, last_there)]
+                last_push = [jnp.where(own_wide, a, b) for a, b in zip(push, last_push)]
+        whole = terms([wide(h, chunks) for h in last_here], last_there, last_push)
+        for c in range(3):
+            value = folded(whole[c][:, : full * ROW]) + jnp.where(
+                lane_at < SEGMENT, whole[c][:, full * ROW :], 0.0
+            )
+            place(result_tail, 8 * c, n, value)
 
     def run_tasks(step):
-        unroll = next(u for u in (3, 2, 1) if slots % u == 0)
-
-        @pl.loop(0, slots // unroll)
+        result_tail[...] = jnp.zeros_like(result_tail)
+
+        @pl.loop(0, quads)
         def _(n):
-            for u in range(unroll):
-                one_slot(step, n * unroll + u)
+            four_slots(step, n)
+
+        even = lax.broadcasted_iota(jnp.int32, (8, ROW), 0) % 2 == 0
+        for c in range(3):
+            block = jnp.zeros((8, ROW), f32)
+            for j in range(4):
+                pair = [
+                    result_tail[8 * c + 2 * j + i : 8 * c + 2 * j + i + 1, :] for i in range(2)
+                ]
+                rows = jnp.where(
+                    even,
+                    jnp.broadcast_to(pair[0], (8, ROW)),
+                    jnp.broadcast_to(pair[1], (8, ROW)),
+                )
+                if j:
+                    rows = pltpu.roll(rows, quads * j, 1)
+                mine = (lane_at >= quads * j) & (lane_at < quads * (j + 1))
+                block = jnp.where(mine, rows, block)
+            at = c * rows_piece + 8 * groups
+            result[at : at + 8, :] = block
 
     def read_tasks():
         targets = task_in[pl.ds(0, lanes, stride=8), :]
@@ -314,6 +416,11 @@
                 whole[c][k] = jnp.where((at >= low) & (at < high), block, whole[c][k])
                 if high > ROW:
                     whole[c][k + 1] = jnp.where(at < high - ROW, block, whole[c][k + 1])
+        for c in range(3):
+            rest = whole[c][full]
+            whole[c][full] = sum(
+                (pltpu.roll(rest, SEGMENT * q, 1) for q in range(1, ROW // SEGMENT)), rest
+            )
         return whole
 
     def lane_copies(source_at, inbox, rows, send, recv):
@@ -336,7 +443,10 @@
     point_of = lax.broadcasted_iota(jnp.int32, (width, ROW), 0) - piece * lane
     mine = jnp.zeros((cells, ROW), f32)
     for c in range(3):
-        pick = (point_of == lane_of - c * rows_piece) & (point_of >= 0) & (point_of < piece)
+        nth = lane_of - c * rows_piece
+        nth = jnp.where(nth < piece, nth, 8 * groups + lax.rem(nth, 2))
+        inside = (lane_of >= c * rows_piece) & (lane_of < (c + 1) * rows_piece)
+        pick = (point_of == nth) & inside
         mine += jnp.dot(
             pool[0, c * pool_cells : c * pool_cells + cells, :],
             pick.astype(f32),
@@ -344,8 +454,14 @@
             preferred_element_type=f32,
         )
     own_slice[...] = mine
+    stage_ghosts(0)
     spread_targets()
-    stage_ghosts(0)
+    loads[5].wait()
+    bend_op = bend_ref[...]
+    for at, value in ((0, bend_op[:, 0 : full * ROW]), (full * ROW, tail(bend_op))):
+        high, low = split_bf16(value)
+        bend_hi[0:points, at : at + value.shape[1]] = high
+        bend_lo[0:points, at : at + value.shape[1]] = low
 
     for core_is in range(2):
         pl.when(core == core_is)(
@@ -460,17 +576,14 @@
     half = owners // 2
     planes = lanes // 2
     f32 = jnp.float32
-    own = jnp.pad(
-        2.0 * jnp.transpose(positions, (1, 0, 2)), ((0, 0), (0, 0), (0, width - points))
-    ).reshape(3 * cells, width)
     vmem = pl.BlockSpec(memory_space=pltpu.VMEM)
-    smem = pl.BlockSpec(memory_space=pltpu.SMEM)
+    hbm = pl.BlockSpec(memory_space=pltpu.HBM)
     dma = pltpu.SemaphoreType.DMA
     out = jax.ShapeDtypeStruct((share, 3, points), f32)
     return pl.pallas_call(
         functools.partial(kernel, (owners, lanes, cells, points, cap, slots)),
         out_shape=(out, out),
-        in_specs=[vmem, vmem, smem, vmem, vmem, vmem],
+        in_specs=[hbm] * 6,
         out_specs=(vmem, vmem),
         scratch_shapes=[
             pltpu.VMEM((ITERS, 3 * pool_cells, width), f32),
@@ -479,7 +592,7 @@
             pltpu.VMEM((width, width), jnp.bfloat16),
             pltpu.VMEM((ITERS, half * box_rows, ROW), f32),
             pltpu.VMEM((ITERS, owners * box_rows, ROW), f32),
-            pltpu.VMEM((cells, cell_rows, ROW), f32),
+            pltpu.VMEM((cells, cell_rows + 24, ROW), f32),
             pltpu.VMEM((ROW, ROW), f32),
             pltpu.VMEM((cells, ROW), f32),
             pltpu.VMEM((cells, ROW), f32),
@@ -501,11 +614,19 @@
             dma((lanes,)),
             dma((lanes,)),
             dma,
+            pltpu.VMEM(positions.shape, f32),
+            pltpu.VMEM(bend_op.shape, f32),
+            pltpu.SMEM(send_list.shape, jnp.int32),
+            pltpu.VMEM((1, cap), jnp.int32),
+            pltpu.VMEM((1, cap), jnp.int32),
+            pltpu.VMEM((1, 1), jnp.int32),
+            dma((6,)),
+            pltpu.VMEM((24, ROW), f32),
         ],
         compiler_params=pltpu.CompilerParams(
             collective_id=0, has_side_effects=True, vmem_limit_bytes=48 * 1024 * 1024
         ),
-    )(own, bend_op, send_list, task_target, task_source, task_count.reshape(1, 1))
+    )(positions, bend_op, send_list, task_target, task_source, task_count.reshape(1, 1))
 
 
 def solution(mesh):

time: 107 us -> 101 us (0.944)
  Pallas kernels: 99.8 us -> 94.2 us
  local copies, waits for them, and re-layouts: 4.54 us -> 5.64 us
    pallas_call x1, Pallas kernels: 99.8 us -> 94.2 us  [shards(): pl.pallas_call(functools.partial(kernel, (owners, lanes, cells, points, c...]
    unnamed x8 -> x9, local copies, waits for them, and re-layouts: 3.3 us -> 4.42 us
where the time goes in v2:
time: 101 us
  Pallas kernels  94.2 us (93%)
  local copies, waits for them, and re-layouts  5.64 us (6%)
  between operations  1.3 us (1%)
    pallas_call x1, Pallas kernels, shards(): pl.pallas_call(functools.partial(kernel, (owners, lanes, cells, points, c...  94.2 us
    unnamed x9, local copies, waits for them, and re-layouts  4.42 us

profile of v2, /device:TPU:1, one launch (start us, length us, event | category | flops | bytes accessed | tf_op | source)
XLA Modules:
  0.0 101.1 jit_solution(9244328016405948848)
XLA Ops:
  1.3 1.1 %copy.8.own_hbm = f32[32,3,544]{2,1,0:T(4,128)S(1)} copy(f32[32,3,544]{2,0,1:T(8,128)} %param.6) | data formatting | bytes 417792 | tf_op args[0]
  2.4 0.0 copy-start
  2.4 1.3 %copy-done = f32[544,544]{1,0:T(8,128)S(1)} copy-done((f32[544,544]{1,0:T(8,128)S(1)}, f32[544,544]{1,0:T(8,128)}, u32[]{:S(2)}) %copy-start) | copy-done | bytes 1183768
  3.7 0.0 copy-start.1
  3.7 0.7 copy-done.1
  4.4 0.0 copy-start.2
  4.4 0.7 copy-done.2
  5.1 0.0 copy-start.3
  5.1 0.7 copy-done.3
  5.7 94.2 %shard_map.77 = (f32[2,3,544]{2,1,0:T(4,128)S(1)}, f32[2,3,544]{2,1,0:T(4,128)S(1)}) custom-call(f32[32,3,544]{2,1,0:T(4,128)S(1)} %copy.8.own_hbm, f32[544,544]{1,0:T(8,128)S(1)} %copy-done, s32[1,64]{1,0:T(1,128)S(1)} %copy-done.1, s32[1,12]{1,0:T(1,128)S(1)} %copy-done.2, s32[1,12]{1,0:T(1,128)S(1)} %copy-done.3, s32[1,1]{1,0:T(1,128)} %bitcast.1.count_hbm), custom_call_target="tpu_custom_call" | custom-call | tf_op jit(solution)/shard_map/pallas_call | solution.py:583
  99.9 0.6 copy.9
  100.5 0.6 copy.10
Async XLA Ops:
  2.4 1.3 %copy-start = (f32[544,544]{1,0:T(8,128)S(1)}, f32[544,544]{1,0:T(8,128)}, u32[]{:S(2)}) copy-start(f32[544,544]{1,0:T(8,128)} %bend_hbm.1) | copy-start | bytes 3551236
  3.7 0.7 copy-start.1
  4.4 0.7 copy-start.2
  5.1 0.7 copy-start.3

commit v3 on v2

--- a/solution.py
+++ b/solution.py
@@ -165,7 +165,7 @@
     loads[3].wait()
     for c in range(3):
         at = c * pool_cells
-        value = 2.0 * own_ref[:, c, :]
+        value = 2.0 * own_ref[c]
         pool[0, at : at + cells, 0 : full * ROW] = value[:, 0 : full * ROW]
         pool[0, at : at + cells, full * ROW :] = tail(value)
     loads[4].wait()
@@ -557,8 +557,8 @@
         speeds = jnp.concatenate(whole[c], axis=1)
         for n in range(share):
             cell = pool[1, pl.ds(c * pool_cells + share * lane + n, 1), :]
-            vel_ref[n, c : c + 1, :] = speeds[n : n + 1, 0:points]
-            moved_ref[n, c : c + 1, :] = (0.5 * (cell + speeds[n : n + 1, :]))[:, 0:points]
+            vel_ref[c, n : n + 1, :] = speeds[n : n + 1, 0:points]
+            moved_ref[c, n : n + 1, :] = (0.5 * (cell + speeds[n : n + 1, :]))[:, 0:points]
 
 
 def shards(owners, lanes, positions, bend_op, send_list, task_target, task_source, task_count):
@@ -579,8 +579,8 @@
     vmem = pl.BlockSpec(memory_space=pltpu.VMEM)
     hbm = pl.BlockSpec(memory_space=pltpu.HBM)
     dma = pltpu.SemaphoreType.DMA
-    out = jax.ShapeDtypeStruct((share, 3, points), f32)
-    return pl.pallas_call(
+    out = jax.ShapeDtypeStruct((3, share, points), f32)
+    moved, velocity = pl.pallas_call(
         functools.partial(kernel, (owners, lanes, cells, points, cap, slots)),
         out_shape=(out, out),
         in_specs=[hbm] * 6,
@@ -614,7 +614,7 @@
             dma((lanes,)),
             dma((lanes,)),
             dma,
-            pltpu.VMEM(positions.shape, f32),
+            pltpu.VMEM((3, cells, points), f32),
             pltpu.VMEM(bend_op.shape, f32),
             pltpu.SMEM(send_list.shape, jnp.int32),
             pltpu.VMEM((1, cap), jnp.int32),
@@ -624,9 +624,17 @@
             pltpu.VMEM((24, ROW), f32),
         ],
         compiler_params=pltpu.CompilerParams(
-            collective_id=0, has_side_effects=True, vmem_limit_bytes=48 * 1024 * 1024
+            collective_id=0, has_side_effects=True, vmem_limit_bytes=67_043_328
         ),
-    )(positions, bend_op, send_list, task_target, task_source, task_count.reshape(1, 1))
+    )(
+        jnp.transpose(positions, (1, 0, 2)),
+        bend_op,
+        send_list,
+        task_target,
+        task_source,
+        task_count.reshape(1, 1),
+    )
+    return jnp.transpose(moved, (1, 0, 2)), jnp.transpose(velocity, (1, 0, 2))
 
 
 def solution(mesh):

time: 101 us -> 99 us (0.980)
  local copies, waits for them, and re-layouts: 5.64 us -> 2.63 us
    unnamed x9 -> x2, local copies, waits for them, and re-layouts: 4.42 us -> 2.63 us
    pallas_call x2 -> x0, local copies, waits for them, and re-layouts: 1.22 us -> none  [shards(): pl.pallas_call(functools.partial(kernel, (owners, lanes, cells, points, c...]
where the time goes in v3:
time: 99 us; the launch traced here: 98.8 us
  Pallas kernels  94.8 us (96%)
  local copies, waits for them, and re-layouts  2.63 us (3%)
  between operations  1.29 us (1%)
    pallas_call x1, Pallas kernels, shards(): pl.pallas_call(functools.partial(kernel, (owners, lanes, cells, points, c...  94.8 us
    unnamed x2, local copies, waits for them, and re-layouts  2.63 us

profile of v3, /device:TPU:1, one launch (start us, length us, event | category | flops | bytes accessed | tf_op | source)
XLA Modules:
  0.0 98.8 jit_solution(13215617310300492999)
XLA Ops:
  1.3 94.8 %shard_map.77 = (f32[3,2,544]{2,1,0:T(2,128)}, f32[3,2,544]{2,1,0:T(2,128)}) custom-call(f32[3,32,544]{2,1,0:T(8,128)} %bitcast.5, f32[544,544]{1,0:T(8,128)} %bend_hbm.1, s32[1,64]{1,0:T(1,128)} %send_hbm.1, s32[1,12]{1,0:T(1,128)} %target_hbm.1, s32[1,12]{1,0:T(1,128)} %source_hbm.1, s32[1,1]{1,0:T(1,128)} %bitcast.4.count_hbm), custom_call_target="tpu_custom_call" | custom-call | tf_op jit(solution)/shard_map/pallas_call | solution.py:583
  96.1 1.3 %copy.11 = f32[2,3,544]{2,0,1:T(2,128)} copy(f32[2,3,544]{2,0,1:T(2,128)} %bitcast.7) | data formatting | bytes 26112
  97.4 1.3 %copy.12 = f32[2,3,544]{2,0,1:T(2,128)} copy(f32[2,3,544]{2,0,1:T(2,128)} %bitcast.6) | data formatting | bytes 26112
